TPU v7x, 32 devices: a whole 2x2x4 slice. The times are simulated.
32 devices in a mesh: ctx: 8 (over z, y), wsh: 4 (over x, core).
Axes of the slice: x: 2, y: 2, z: 4, core: 2. Of those that a mesh axis runs over, the one named last changes fastest.
Arguments:
- tokens: bfloat16 [4, 1024, 2048], P('wsh', 'ctx'), may hold values from -6 to 6
- out_grad: bfloat16 [4, 1024, 2048], P('wsh', 'ctx'), may hold values from -6 to 6
- attn_weight: bfloat16 [4, 2048, 2048], P(None, None, 'wsh'), may hold values from -0.125 to 0.125
- mlp_weight: bfloat16 [3, 2048, 8192], P(None, None, 'wsh'), may hold values from -0.125 to 0.125
- norm_gains: bfloat16 [4, 2048], P(None, 'wsh'), may hold values from 0.25 to 1.75
- adapt_model: bfloat16 [11, 64, 2048], P(None, None, 'wsh'), may hold values from -0.125 to 0.125
- adapt_hidden: bfloat16 [3, 64, 8192], P(None, None, 'wsh'), may hold values from -0.0625 to 0.0625
- lengths: int32 [4], replicated, may hold values from 512 to 1024, as said below
- adapter_pick: int32 [4], replicated, may hold values from 0 to 3
- block_order: int32 [4, 16], P('wsh'), may hold values from 0 to 15, as said below
Outputs:
- layer_out: bfloat16 [4, 1024, 2048], P('wsh', 'ctx')
- input_grad: float32 [4, 1024, 2048], P('wsh', 'ctx')
- adapt_model_grad: float32 [11, 64, 2048], P(None, None, 'wsh')
- adapt_hidden_grad: float32 [3, 64, 8192], P(None, None, 'wsh')
Inputs may be any that keep to these rules, and one draw needn't show every extreme that they name: `lengths`: some sequence has exactly 1024 valid tokens. Each row of block_order is a permutation of the 16 blocks; the two blocks stored on one index of ctx are p and 15 - p for some p, in either order.
All inputs are finite; a program needn't handle non-finite values.
Results may differ from a plain program's by a relative error of at most 0.017.
Values may be sent and summed in bfloat16 or wider, within the bound.
No kernel may reach another device: no remote copies, remote signals or barrier semaphores. Data moves between devices by JAX's collectives and lax.ppermute only.
A program may use at most 512 MiB of HBM per device.

v0:
```python
import math
import jax
import jax.numpy as jnp
from jax import lax
from jax.sharding import PartitionSpec as P

HEADS = 16
HEAD_DIM = 128
RANK = 16
ADAPTERS = 4
NORM_EPS = 1e-06
ADAPTER_SCALE = 4.0
ROPE_BASE = 500000.0
F32 = jnp.float32
BF16 = jnp.bfloat16
CORE_SWAP = ((0, 1), (1, 0), (2, 3), (3, 2))
CHIP_SWAP = ((0, 2), (2, 0), (1, 3), (3, 1))


def dot(left, right, dims):
    return lax.dot_general(left, right, (dims, ((), ())), preferred_element_type=F32)


def mm(left, right):
    return dot(left, right, ((1,), (0,)))


def mm_t(left, right):
    return dot(left, right, ((1,), (1,)))


def tmm(left, right):
    return dot(left, right, ((0,), (0,)))


def swap_core(values):
    return lax.ppermute(values, "wsh", CORE_SWAP)


def swap_chip(values):
    return lax.ppermute(values, "wsh", CHIP_SWAP)


def sum_wsh(values):
    values = values + swap_core(values)
    return values + swap_chip(values)


def gather_wsh(block, axis, me):
    far = swap_chip(block)
    near = swap_core(block)
    far_near = swap_core(far)
    extent = block.shape[axis]
    shape = list(block.shape)
    shape[axis] = 4 * extent
    whole = jnp.zeros(shape, block.dtype)
    for flip, piece in ((0, block), (1, near), (2, far), (3, far_near)):
        start = [0] * block.ndim
        start[axis] = (me ^ flip) * extent
        whole = lax.dynamic_update_slice(whole, piece, start)
    return whole


def scatter_wsh(partial, axis, me):
    extent = partial.shape[axis] // 4

    def piece(flip):
        return lax.dynamic_slice_in_dim(partial, (me ^ flip) * extent, extent, axis)

    far = piece(2).astype(F32) + swap_core(piece(3)).astype(F32)
    far = swap_chip(far.astype(BF16))
    near = piece(0).astype(F32) + swap_core(piece(1)).astype(F32)
    return near + far.astype(F32)


def rotate(values, cosine, sine_part):
    half = HEAD_DIM // 2
    first, second = (values[..., :half], values[..., half:])
    return jnp.concatenate(
        [first * cosine - second * sine_part, second * cosine + first * sine_part], axis=-1
    )


def per_device(
    tokens,
    out_grad,
    attn_weight,
    mlp_weight,
    norm_gains,
    adapt_model,
    adapt_hidden,
    lengths,
    adapter_pick,
    block_order,
):
    own_rows = tokens[0]
    rows, model_dim = own_rows.shape
    block_rows = rows // 2
    ctx_size = lax.axis_size("ctx")
    seqs = lax.axis_size("wsh")
    width = model_dim // seqs
    local_heads = width // HEAD_DIM
    me = lax.axis_index("wsh")
    ctx_index = lax.axis_index("ctx")
    pairs = seqs * local_heads
    members = math.gcd(ctx_size, pairs)
    groups = ctx_size // members
    per_member = pairs // members
    splits = local_heads // per_member
    group_rows = members * rows
    member = ctx_index % members
    group = ctx_index // members
    ctx_groups = [[g * members + i for i in range(members)] for g in range(groups)]
    key_groups = [[g * members + i for g in range(groups)] for i in range(members)]
    score_scale = HEAD_DIM ** (-0.5)
    all_rows = seqs * rows

    def columns(matrix):
        return lax.dynamic_slice_in_dim(matrix, me * width, width, 1)

    orders = gather_wsh(block_order, 0, me)
    positions = (orders[:, :, None] * block_rows + jnp.arange(block_rows)[None, None, :]).reshape(
        seqs, -1
    )
    row_positions = lax.dynamic_slice_in_dim(positions, ctx_index * rows, rows, 1)
    own_positions = lax.dynamic_index_in_dim(row_positions, me, keepdims=False)
    own_length = lax.dynamic_index_in_dim(lengths, me, keepdims=False)
    valid_rows = (own_positions < own_length).astype(F32)[:, None]
    half_dim = HEAD_DIM // 2
    frequency = ROPE_BASE ** (-(jnp.arange(half_dim, dtype=F32) * 2.0) / HEAD_DIM)
    angles = row_positions.reshape(-1).astype(F32)[:, None] * frequency[None, :]
    cosine, sine_part = (jnp.cos(angles)[:, None, :], jnp.sin(angles)[:, None, :])
    picked = (jnp.arange(ADAPTERS * RANK)[None, :] // RANK == adapter_pick[:, None]).astype(F32)
    row_mask = jnp.broadcast_to(picked[:, None, :], (seqs, rows, ADAPTERS * RANK)).reshape(
        all_rows, -1
    )

    def low(product):
        return (product * row_mask).astype(BF16)

    def low_sum(partial):
        narrow = (partial * row_mask).reshape(all_rows, ADAPTERS, RANK).sum(1)
        total = jnp.tile(sum_wsh(narrow), (1, ADAPTERS))
        return (total * row_mask).astype(BF16)

    gains = norm_gains.astype(F32)
    last_gain = gather_wsh(norm_gains[3:4], 1, me).astype(F32)
    hidden = gather_wsh(own_rows, 0, me)
    rows_a = gather_wsh(jnp.concatenate([adapt_model[:6], adapt_model[10:11]], 0), 2, me)
    low_in = [low(mm_t(hidden, rows_a[k])) for k in range(3)]
    proj = [
        mm(hidden, attn_weight[k]) + ADAPTER_SCALE * mm(low_in[k], adapt_model[6 + k])
        for k in range(3)
    ]
    squares = jnp.stack([jnp.sum(proj[0] * proj[0], -1), jnp.sum(proj[1] * proj[1], -1)])
    scales = lax.rsqrt(sum_wsh(squares) / model_dim + NORM_EPS)[:, :, None]

    def heads(values):
        return values.reshape(all_rows, local_heads, HEAD_DIM)

    turned = [
        rotate(heads(proj[k] * scales[k] * gains[k]), cosine, sine_part).astype(BF16)
        for k in range(2)
    ]
    packed = jnp.stack([turned[0], turned[1], heads(proj[2].astype(BF16))])

    def to_heads(values):
        count = values.shape[0]
        shaped = values.reshape(count, seqs, rows, splits, per_member * HEAD_DIM)
        shaped = shaped.transpose(1, 3, 0, 2, 4).reshape(
            members, count, rows, per_member * HEAD_DIM
        )
        moved = lax.all_to_all(shaped, "ctx", 0, 0, tiled=True, axis_index_groups=ctx_groups)
        moved = moved.transpose(1, 0, 2, 3).reshape(count, group_rows, per_member, HEAD_DIM)
        return moved.transpose(0, 2, 1, 3)

    def to_rows(values):
        count = values.shape[0]
        shaped = values.transpose(0, 2, 1, 3).reshape(count, members, rows, per_member * HEAD_DIM)
        moved = lax.all_to_all(
            shaped.transpose(1, 0, 2, 3), "ctx", 0, 0, tiled=True, axis_index_groups=ctx_groups
        )
        moved = moved.reshape(seqs, splits, count, rows, per_member * HEAD_DIM)
        return moved.transpose(2, 0, 3, 1, 4).reshape(count, all_rows, width)

    queries, keys, values = to_heads(packed)
    if groups > 1:
        keys, values = (
            lax.all_gather(part, "ctx", axis=1, tiled=True, axis_index_groups=key_groups)
            for part in (keys, values)
        )
    seq_here = member * per_member // local_heads
    key_positions = lax.dynamic_index_in_dim(positions, seq_here, keepdims=False)
    query_positions = lax.dynamic_slice_in_dim(key_positions, group * group_rows, group_rows)
    length_here = lax.dynamic_index_in_dim(lengths, seq_here, keepdims=False)
    allowed = (key_positions[None, :] <= query_positions[:, None]) & (
        key_positions[None, :] < length_here
    )

    def batched(left, right, lc, rc):
        return lax.dot_general(
            left, right, (((lc,), (rc,)), ((0,), (0,))), preferred_element_type=F32
        )

    scores = jnp.where(allowed[None], batched(queries, keys, 2, 2) * score_scale, -jnp.inf)
    row_max = jnp.max(scores, axis=-1, keepdims=True)
    log_total = row_max + jnp.log(jnp.sum(jnp.exp(scores - row_max), axis=-1, keepdims=True))
    weights = jnp.exp(scores - log_total).astype(BF16)
    attended = batched(weights, values, 2, 1).astype(BF16)
    attended = to_rows(attended[None])[0]
    attended_full = gather_wsh(attended, 1, me)
    low_out = low(mm_t(attended_full, rows_a[3]))
    branch = mm(attended_full, attn_weight[3]) + ADAPTER_SCALE * mm(low_out, adapt_model[9])
    branch_scale = lax.rsqrt(
        sum_wsh(jnp.sum(branch * branch, -1, keepdims=True)) / model_dim + NORM_EPS
    )
    mid = columns(hidden).astype(F32) + branch * branch_scale * gains[2]
    mid_low = mid.astype(BF16)
    mid_full = gather_wsh(mid_low, 1, me)
    low_gate = low(mm_t(mid_full, rows_a[4]))
    low_up = low(mm_t(mid_full, rows_a[5]))
    gate = mm(mid_full, mlp_weight[0]) + ADAPTER_SCALE * mm(low_gate, adapt_hidden[0])
    up = mm(mid_full, mlp_weight[1]) + ADAPTER_SCALE * mm(low_up, adapt_hidden[1])
    sigmoid_gate = jax.nn.sigmoid(gate)
    silu_gate = gate * sigmoid_gate
    product = (silu_gate * up).astype(BF16)
    low_down_part = mm_t(product, adapt_hidden[2])
    down_part = mm_t(product, mlp_weight[2]) + ADAPTER_SCALE * mm(low(low_down_part), rows_a[6])
    down = scatter_wsh(down_part.astype(BF16), 0, me)
    low_down = low_sum(low_down_part)
    down_scale = lax.rsqrt(jnp.mean(down * down, axis=-1, keepdims=True) + NORM_EPS)
    mid_rows = lax.dynamic_slice_in_dim(mid_full, me * rows, rows, 0).astype(F32)
    result = mid_rows + down * down_scale * last_gain
    upstream = out_grad[0].astype(F32) * valid_rows
    scaled = upstream * last_gain
    grad_down = (
        down_scale * scaled - down * down_scale**3 * jnp.mean(scaled * down, axis=-1, keepdims=True)
    ).astype(BF16)
    grad_down = gather_wsh(grad_down, 0, me)
    grad_low_down = low(ADAPTER_SCALE * mm_t(grad_down, rows_a[6]))
    grad_product = mm(grad_down, mlp_weight[2]) + mm(grad_low_down, adapt_hidden[2])
    grad_gate = (grad_product * up * sigmoid_gate * (1.0 + gate * (1.0 - sigmoid_gate))).astype(
        BF16
    )
    grad_up = (grad_product * silu_gate).astype(BF16)
    low_gate_part = ADAPTER_SCALE * mm_t(grad_gate, adapt_hidden[0])
    low_up_part = ADAPTER_SCALE * mm_t(grad_up, adapt_hidden[1])
    own_block = (jnp.arange(seqs) == me).astype(F32)[:, None, None]
    mid_part = (
        mm_t(grad_gate, mlp_weight[0])
        + mm_t(grad_up, mlp_weight[1])
        + mm(low(low_gate_part), rows_a[4])
        + mm(low(low_up_part), rows_a[5])
        + (own_block * upstream[None]).reshape(all_rows, model_dim)
    )
    grad_mid = scatter_wsh(mid_part.astype(BF16), 1, me)
    grad_low_gate = low_sum(low_gate_part)
    grad_low_up = low_sum(low_up_part)
    hidden_grads = jnp.stack(
        [
            ADAPTER_SCALE * tmm(low_gate, grad_gate),
            ADAPTER_SCALE * tmm(low_up, grad_up),
            tmm(grad_low_down, product),
        ]
    )
    grad_a_gate = tmm(grad_low_gate, mid_low)
    grad_a_up = tmm(grad_low_up, mid_low)
    grad_b_down = ADAPTER_SCALE * tmm(low_down, columns(grad_down))
    scaled = grad_mid * gains[2]
    mean = sum_wsh(jnp.sum(scaled * branch, axis=-1, keepdims=True)) / model_dim
    grad_branch = (branch_scale * scaled - branch * branch_scale**3 * mean).astype(BF16)
    low_out_part = ADAPTER_SCALE * mm_t(grad_branch, adapt_model[9])
    attended_part = mm_t(grad_branch, attn_weight[3]) + mm(low(low_out_part), rows_a[3])
    grad_attended = scatter_wsh(attended_part.astype(BF16), 1, me).astype(BF16)
    grad_low_out = low_sum(low_out_part)
    grad_b_out = ADAPTER_SCALE * tmm(low_out, grad_branch)
    grad_a_out = tmm(grad_low_out, attended)
    grad_heads = to_heads(grad_attended[None])[0]
    scores = jnp.where(allowed[None], batched(queries, keys, 2, 2) * score_scale, -jnp.inf)
    weights_full = jnp.exp(scores - log_total)
    grad_probs = batched(grad_heads, values, 2, 2)
    delta = jnp.sum(weights_full * grad_probs, axis=-1, keepdims=True)
    grad_scores = (weights_full * (grad_probs - delta)).astype(BF16)
    grad_queries = batched(grad_scores, keys, 2, 1) * score_scale
    grad_keys = batched(grad_scores, queries, 1, 1) * score_scale
    grad_values = batched(weights_full.astype(BF16), grad_heads, 1, 1)
    if groups > 1:
        grad_keys, grad_values = (
            lax.psum_scatter(
                part, "ctx", scatter_dimension=1, tiled=True, axis_index_groups=key_groups
            )
            for part in (grad_keys, grad_values)
        )
    grads = to_rows(jnp.stack([grad_queries, grad_keys, grad_values]).astype(BF16))
    turned = [
        rotate(heads(grads[k].astype(F32)), cosine, -sine_part).reshape(all_rows, width) * gains[k]
        for k in range(2)
    ]
    sums = jnp.stack([jnp.sum(turned[k] * proj[k], -1) for k in range(2)])
    means = (sum_wsh(sums) / model_dim)[:, :, None]
    grad_proj = [
        (scales[k] * turned[k] - proj[k] * scales[k] ** 3 * means[k]).astype(BF16) for k in range(2)
    ] + [grads[2]]
    low_parts = [ADAPTER_SCALE * mm_t(grad_proj[k], adapt_model[6 + k]) for k in range(3)]
    own_column = (jnp.arange(seqs) == me).astype(F32)[None, :, None]
    input_part = (
        mm_t(grad_proj[0], attn_weight[0])
        + mm_t(grad_proj[1], attn_weight[1])
        + mm_t(grad_proj[2], attn_weight[2])
        + mm(low(low_parts[0]), rows_a[0])
        + mm(low(low_parts[1]), rows_a[1])
        + mm(low(low_parts[2]), rows_a[2])
        + (own_column * grad_mid[:, None, :]).reshape(all_rows, model_dim)
    )
    grad_inputs = scatter_wsh(input_part.astype(BF16), 0, me)
    own_hidden = columns(hidden)
    grad_a_in = [tmm(low_sum(low_parts[k]), own_hidden) for k in range(3)]
    grad_b_in = [ADAPTER_SCALE * tmm(low_in[k], grad_proj[k]) for k in range(3)]
    model_grads = jnp.stack(
        grad_a_in + [grad_a_out, grad_a_gate, grad_a_up] + grad_b_in + [grad_b_out, grad_b_down]
    )
    model_grads = lax.psum(model_grads, "ctx")
    hidden_grads = lax.psum(hidden_grads, "ctx")
    return (result.astype(BF16)[None], grad_inputs[None], model_grads, hidden_grads)


def solution(mesh):
    in_specs = (
        P("wsh", "ctx", None),
        P("wsh", "ctx", None),
        P(None, None, "wsh"),
        P(None, None, "wsh"),
        P(None, "wsh"),
        P(None, None, "wsh"),
        P(None, None, "wsh"),
        P(),
        P(),
        P("wsh", None),
    )
    out_specs = (
        P("wsh", "ctx", None),
        P("wsh", "ctx", None),
        P(None, None, "wsh"),
        P(None, None, "wsh"),
    )
    return jax.shard_map(
        per_device, mesh=mesh, in_specs=in_specs, out_specs=out_specs, check_vma=False
    )
```

profile of v0, /device:TPU:0, one launch (start us, length us, event | category | flops | bytes accessed | tf_op | source)
XLA Modules:
  0.0 655.7 jit_solution(950616927271443762)
XLA Ops:
  7.2 3.0 collective-permute-start.4
  20.7 15.3 %collective-permute-done.7 = bf16[7,64,512]{2,1,0:T(8,128)(2,1)} collective-permute-done((bf16[7,64,512]{2,1,0:T(8,128)(2,1)}, bf16[7,64,512]{2,1,0:T(8,128)(2,1)}, u32[]{:S(2)}, u32[]{:S(2)}) %collective-permute-start.7) | collective-permute-done | bytes 458784 | tf_op jit(solution)/shard_map/ppermute | solution.py:41
  64.8 3.7 maximum_bitcast_fusion
  68.4 3.7 copy.160
  72.2 6.4 all-to-all-start
  81.7 34.0 %all-to-all-done = bf16[8,3,128,256]{3,2,1,0:T(8,128)(2,1)} async-done(((bf16[8,3,128,256]{3,2,1,0:T(8,128)(2,1)}), bf16[8,3,128,256]{3,2,1,0:T(8,128)(2,1)}, u32[]{:S(2)}, u32[]{:S(2)}) %all-to-all-start) | async-done | bytes 1572896 | tf_op jit(solution)/shard_map/all_to_all | solution.py:173
  115.7 2.8 copy.161
  118.4 3.7 reshape.481
  122.1 2.6 copy.162
  124.7 3.0 fusion.18
  131.0 4.8 fusion.75
  139.1 18.4 %all_to_all.20 = bf16[8,1,128,256]{2,3,1,0:T(8,128)(2,1)} all-to-all(bf16[8,1,128,256]{2,3,1,0:T(8,128)(2,1)S(1)} %copy.165), channel_id=1, replica_groups={{0,4,8,12,16,20,24,28},{1,5,9,13,17,21,25,29},{2,6,10,14,18,22,26,30},{..., dimensions={0} | all-to-all | bytes 1048576 | tf_op jit(solution)/shard_map/all_to_all | solution.py:180
  164.5 11.0 %collective-permute-done.12 = bf16[512,512]{0,1:T(8,128)(2,1)S(1)} collective-permute-done((bf16[512,512]{0,1:T(8,128)(2,1)S(1)}, bf16[512,512]{0,1:T(8,128)(2,1)S(1)}, u32[]{:S(2)}, u32[]{:S(2)}) %collective-permute-start.12) | collective-permute-done | bytes 524320 | tf_op jit(solution)/shard_map/ppermute | solution.py:41
  179.2 2.9 multiply_reduce_fusion.5
  189.8 11.3 %collective-permute-done.17 = bf16[512,512]{0,1:T(8,128)(2,1)S(1)} collective-permute-done((bf16[512,512]{0,1:T(8,128)(2,1)S(1)}, bf16[512,512]{0,1:T(8,128)(2,1)S(1)}, u32[]{:S(2)}, u32[]{:S(2)}) %collective-permute-start.17) | collective-permute-done | bytes 524320 | tf_op jit(solution)/shard_map/ppermute | solution.py:41
  207.7 11.6 %multiply_add_fusion.1 = f32[512,2048]{0,1:T(8,128)} fusion(f32[512,2048]{0,1:T(8,128)S(1)} %fusion.137, bf16[512,2048]{0,1:T(8,128)(2,1)S(1)} %constant_dynamic-update-slice_fusion.4, bf16[3,2048,2048]{2,1,0:T(8,128)(2,1)} %param.13), kind=kOutput, calls=%fused_computation.37 | convolution fusion | flops 4297064448 | bytes 18874368 | tf_op jit(solution)/shard_map/dot_general | solution.py:21
  219.3 13.1 %multiply_convert_fusion.3 = (bf16[512,2048]{0,1:T(8,128)(2,1)S(1)}, f32[512,2048]{0,1:T(8,128)}) fusion(f32[512,2048]{0,1:T(8,128)} %multiply_add_fusion.1, f32[512,2048]{0,1:T(8,128)S(1)} %fusion.134, bf16[512,2048]{0,1:T(8,128)(2,1)S(1)} %constant_dynamic-update-slice_fusion.4, bf16[3,2048,2048]{2,1,0:T(8,128)(2,1)} %param.13), kind=kOutput, calls=%fused_computation.33 | convolution fusion | flops 4303355904 | bytes 25165824 | tf_op jit(solution)/shard_map/dot_general | solution.py:21
  232.9 7.1 %fusion.2 = f32[512,2048]{0,1:T(8,128)S(1)} fusion(bf16[512,2048]{0,1:T(8,128)(2,1)S(1)} %get-tuple-element.95, bf16[3,2048,2048]{2,1,0:T(8,128)(2,1)} %param.13), kind=kOutput, calls=%fused_computation.2 | convolution fusion | flops 4294967296 | bytes 14680064 | tf_op jit(solution)/shard_map/dot_general | solution.py:21
  250.0 10.0 %collective-permute-done.23 = bf16[1,512]{1,0:T(2,128)(2,1)S(1)} collective-permute-done((bf16[1,512]{1,0:T(2,128)(2,1)S(1)}, bf16[1,512]{1,0:T(2,128)(2,1)S(1)}, u32[]{:S(2)}, u32[]{:S(2)}) %collective-permute-start.23) | collective-permute-done | bytes 1056 | tf_op jit(solution)/shard_map/ppermute | solution.py:41
  268.0 12.4 %collective-permute-done.26 = bf16[128,2048]{0,1:T(8,128)(2,1)S(1)} collective-permute-done((bf16[128,2048]{0,1:T(8,128)(2,1)S(1)}, bf16[128,2048]{0,1:T(8,128)(2,1)S(1)}, u32[]{:S(2)}, u32[]{:S(2)}) %collective-permute-start.26) | collective-permute-done | bytes 524320 | tf_op jit(solution)/shard_map/ppermute | solution.py:41
  284.9 10.0 %multiply_convert_fusion.1 = (bf16[512,2048]{0,1:T(8,128)(2,1)S(1)}, bf16[512,2048]{0,1:T(8,128)(2,1)S(1)}) fusion(f32[512,2048]{0,1:T(8,128)} %multiply_add_fusion.1, f32[512,2048]{0,1:T(8,128)} %get-tuple-element.96, f32[512,2048]{0,1:T(8,128)S(1)} %fusion.130, bf16[512,2048]{0,1:T(8,128)(2,1)S(1)} %constant_dynamic-update-slice_fusion, ...), kind=kOutput, calls=%fused_computation.30 | convolution fusion | flops 4309647360 | bytes 27262976 | tf_op jit(solution)/shard_map/dot_general | solution.py:21
  295.4 7.9 %fusion.8 = f32[512,2048]{0,1:T(8,128)S(1)} fusion(bf16[512,2048]{0,1:T(8,128)(2,1)S(1)} %get-tuple-element.39, bf16[3,2048,2048]{2,1,0:T(8,128)(2,1)} %param.13), kind=kOutput, calls=%fused_computation.8 | convolution fusion | flops 4294967296 | bytes 14680064 | tf_op jit(solution)/shard_map/dot_general | solution.py:21
  303.8 6.9 %fusion.4 = f32[512,2048]{0,1:T(8,128)S(1)} fusion(bf16[512,2048]{0,1:T(8,128)(2,1)S(1)} %get-tuple-element.38, bf16[3,2048,2048]{2,1,0:T(8,128)(2,1)} %param.13), kind=kOutput, calls=%fused_computation.4 | convolution fusion | flops 4294967296 | bytes 14680064 | tf_op jit(solution)/shard_map/dot_general | solution.py:21
  319.4 12.4 %collective-permute-done.30 = bf16[512,512]{0,1:T(8,128)(2,1)S(1)} collective-permute-done((bf16[512,512]{0,1:T(8,128)(2,1)S(1)}, bf16[512,512]{0,1:T(8,128)(2,1)S(1)}, u32[]{:S(2)}, u32[]{:S(2)}) %collective-permute-start.30) | collective-permute-done | bytes 524320 | tf_op jit(solution)/shard_map/ppermute | solution.py:41
  337.5 2.9 fusion.32
  346.0 12.4 %collective-permute-done.35 = bf16[512,512]{1,0:T(8,128)(2,1)S(1)} collective-permute-done((bf16[512,512]{1,0:T(8,128)(2,1)S(1)}, bf16[512,512]{1,0:T(8,128)(2,1)S(1)}, u32[]{:S(2)}, u32[]{:S(2)}) %collective-permute-start.35) | collective-permute-done | bytes 524320 | tf_op jit(solution)/shard_map/ppermute | solution.py:41
  362.5 18.6 %all_to_all.21 = bf16[8,1,128,256]{3,2,1,0:T(8,128)(2,1)} all-to-all(bf16[8,1,128,256]{3,2,1,0:T(8,128)(2,1)S(1)} %bitcast.544), channel_id=1, replica_groups={{0,4,8,12,16,20,24,28},{1,5,9,13,17,21,25,29},{2,6,10,14,18,22,26,30},{..., dimensions={0} | all-to-all | bytes 1048576 | tf_op jit(solution)/shard_map/all_to_all | solution.py:173
  383.1 5.5 fusion.76
  388.6 5.5 multiply_reduce_fusion
  394.1 2.7 multiply_convert_fusion
  401.2 2.6 copy.186
  407.2 4.5 all-to-all-start.3
  419.7 3.2 convolution_bitcast_fusion
  438.5 4.0 copy.219
  443.1 4.7 all-to-all-done.3
  447.8 2.6 copy.188
  450.4 2.9 fusion.192
  456.5 2.6 reshape.499
  461.7 2.6 reshape.498
  470.0 5.0 fusion.36
  481.6 5.1 fusion.40
  488.7 4.9 fusion.44
  496.2 3.8 fusion.139
  505.3 3.7 fusion.140
  520.6 10.5 %add_convert_fusion = bf16[512,2048]{1,0:T(8,128)(2,1)S(1)} fusion(f32[512,2048]{1,0:T(8,128)} %bitcast.518, f32[512,2048]{1,0:T(8,128)} %fusion.140, f32[512,2048]{1,0:T(8,128)} %fusion.139, f32[512,2048]{1,0:T(8,128)} %fusion.36, f32[512,2048]{1,0:T(8,128)} %fusion.44, f32[512,2048]{1,0:T(8,128)} %fusion.40, f32[2048]{0:T(1024)S(1)} %bitcast.557, ...), kind=kOutput, calls=%fused_computation.28 | convolution fusion | flops 142639104 | bytes 27664384 | tf_op jit(solution)/shard_map/dot_general | solution.py:21
  537.7 10.7 %collective-permute-done.40 = bf16[128,2048]{1,0:T(8,128)(2,1)} collective-permute-done((bf16[128,2048]{1,0:T(8,128)(2,1)S(1)}, bf16[128,2048]{1,0:T(8,128)(2,1)}, u32[]{:S(2)}, u32[]{:S(2)}) %collective-permute-start.40) | collective-permute-done | bytes 524320 | tf_op jit(solution)/shard_map/ppermute | solution.py:41
  551.0 93.8 %all-reduce.3.cloned.1.call-done = (f32[11,64,512]{2,1,0:T(8,128)}, f32[3,64,2048]{2,1,0:T(8,128)}) async-done(((f32[11,64,512]{2,1,0:T(8,128)}, f32[3,64,2048]{2,1,0:T(8,128)}), (f32[11,64,512]{2,1,0:T(8,128)}, f32[3,64,2048]{2,1,0:T(8,128)})) %all-reduce.3.cloned.1.call-update) | async-done | bytes 3014672 | tf_op jit(solution)/shard_map/psum | solution.py:322
  644.8 2.7 copy.296
  (519 shorter events, 204.1 us)
Async XLA Ops:
  7.2 10.8 %collective-permute-start.4 = (s32[1,16]{1,0:T(1,128)}, s32[1,16]{1,0:T(1,128)S(1)}, u32[]{:S(2)}, u32[]{:S(2)}) collective-permute-start(s32[1,16]{1,0:T(1,128)} %param.19), channel_id=1, source_target_pairs={{0,2},{2,0},{1,3},{3,1},{4,6},{6,4},{5,7},{7,5},{8,10},{10,8},{9,1... | collective-permute-start | bytes 200 | tf_op jit(solution)/shard_map/ppermute | solution.py:41
  10.2 5.8 collective-permute-start.3
  11.5 27.8 %collective-permute-start = (bf16[128,2048]{0,1:T(8,128)(2,1)S(1)}, bf16[128,2048]{0,1:T(8,128)(2,1)}, u32[]{:S(2)}, u32[]{:S(2)}) collective-permute-start(bf16[128,2048]{0,1:T(8,128)(2,1)S(1)} %bitcast.539), channel_id=1, source_target_pairs={{0,1},{1,0},{2,3},{3,2},{4,5},{5,4},{6,7},{7,6},{8,9},{9,8},{10,11... | collective-permute-start | bytes 1572872 | tf_op jit(solution)/shard_map/ppermute | solution.py:37
  12.1 26.7 %collective-permute-start.1 = (bf16[128,2048]{0,1:T(8,128)(2,1)S(1)}, bf16[128,2048]{0,1:T(8,128)(2,1)}, u32[]{:S(2)}, u32[]{:S(2)}) collective-permute-start(bf16[128,2048]{0,1:T(8,128)(2,1)S(1)} %bitcast.540), channel_id=1, source_target_pairs={{0,2},{2,0},{1,3},{3,1},{4,6},{6,4},{5,7},{7,5},{8,10},{10,8},{9,1... | collective-permute-start | bytes 1572872 | tf_op jit(solution)/shard_map/ppermute | solution.py:41
  14.7 21.3 %collective-permute-start.6 = (bf16[7,64,512]{2,1,0:T(8,128)(2,1)}, bf16[7,64,512]{2,1,0:T(8,128)(2,1)S(1)}, u32[]{:S(2)}, u32[]{:S(2)}) collective-permute-start(bf16[7,64,512]{2,1,0:T(8,128)(2,1)} %get-tuple-element.59), channel_id=1, source_target_pairs={{0,1},{1,0},{2,3},{3,2},{4,5},{5,4},{6,7},{7,6},{8,9},{9,8},{10,11... | collective-permute-start | bytes 1376264 | tf_op jit(solution)/shard_map/ppermute | solution.py:37
  16.0 20.0 %collective-permute-start.7 = (bf16[7,64,512]{2,1,0:T(8,128)(2,1)}, bf16[7,64,512]{2,1,0:T(8,128)(2,1)}, u32[]{:S(2)}, u32[]{:S(2)}) collective-permute-start(bf16[7,64,512]{2,1,0:T(8,128)(2,1)} %get-tuple-element.59), channel_id=1, source_target_pairs={{0,2},{2,0},{1,3},{3,1},{4,6},{6,4},{5,7},{7,5},{8,10},{10,8},{9,1... | collective-permute-start | bytes 1376264 | tf_op jit(solution)/shard_map/ppermute | solution.py:41
  36.0 5.8 collective-permute-start.8
  38.8 3.8 collective-permute-start.2
  54.0 4.3 collective-permute-start.10
  72.2 43.5 %all-to-all-start = ((bf16[8,3,128,256]{3,2,1,0:T(8,128)(2,1)}), bf16[8,3,128,256]{3,2,1,0:T(8,128)(2,1)}, u32[]{:S(2)}, u32[]{:S(2)}) async-start(bf16[8,3,128,256]{3,2,1,0:T(8,128)(2,1)} %bitcast.528), calls=%async_computation | async-start | bytes 3145728 | tf_op jit(solution)/shard_map/all_to_all | solution.py:173
  162.8 12.7 %collective-permute-start.12 = (bf16[512,512]{0,1:T(8,128)(2,1)S(1)}, bf16[512,512]{0,1:T(8,128)(2,1)S(1)}, u32[]{:S(2)}, u32[]{:S(2)}) collective-permute-start(bf16[512,512]{0,1:T(8,128)(2,1)S(1)} %bitcast.553), channel_id=1, source_target_pairs={{0,2},{2,0},{1,3},{3,1},{4,6},{6,4},{5,7},{7,5},{8,10},{10,8},{9,1... | collective-permute-start | bytes 1572872 | tf_op jit(solution)/shard_map/ppermute | solution.py:41
  164.5 11.3 %collective-permute-start.11 = (bf16[512,512]{0,1:T(8,128)(2,1)S(1)}, bf16[512,512]{0,1:T(8,128)(2,1)S(1)}, u32[]{:S(2)}, u32[]{:S(2)}) collective-permute-start(bf16[512,512]{0,1:T(8,128)(2,1)S(1)} %bitcast.554), channel_id=1, source_target_pairs={{0,1},{1,0},{2,3},{3,2},{4,5},{5,4},{6,7},{7,6},{8,9},{9,8},{10,11... | collective-permute-start | bytes 1572872 | tf_op jit(solution)/shard_map/ppermute | solution.py:37
  183.4 3.6 collective-permute-start.15
  188.2 12.8 %collective-permute-start.17 = (bf16[512,512]{0,1:T(8,128)(2,1)S(1)}, bf16[512,512]{0,1:T(8,128)(2,1)S(1)}, u32[]{:S(2)}, u32[]{:S(2)}) collective-permute-start(bf16[512,512]{0,1:T(8,128)(2,1)S(1)} %get-tuple-element.35), channel_id=1, source_target_pairs={{0,2},{2,0},{1,3},{3,1},{4,6},{6,4},{5,7},{7,5},{8,10},{10,8},{9,1... | collective-permute-start | bytes 1572872 | tf_op jit(solution)/shard_map/ppermute | solution.py:41
  189.8 11.3 %collective-permute-start.16 = (bf16[512,512]{0,1:T(8,128)(2,1)S(1)}, bf16[512,512]{0,1:T(8,128)(2,1)S(1)}, u32[]{:S(2)}, u32[]{:S(2)}) collective-permute-start(bf16[512,512]{0,1:T(8,128)(2,1)S(1)} %get-tuple-element.35), channel_id=1, source_target_pairs={{0,1},{1,0},{2,3},{3,2},{4,5},{5,4},{6,7},{7,6},{8,9},{9,8},{10,11... | collective-permute-start | bytes 1572872 | tf_op jit(solution)/shard_map/ppermute | solution.py:37
  242.9 19.3 %collective-permute-start.19 = (bf16[128,2048]{0,1:T(8,128)(2,1)}, bf16[128,2048]{0,1:T(8,128)(2,1)}, u32[]{:S(2)}, u32[]{:S(2)}) collective-permute-start(bf16[128,2048]{0,1:T(8,128)(2,1)} %get-tuple-element.46), channel_id=1, source_target_pairs={{0,1},{1,0},{2,3},{3,2},{4,5},{5,4},{6,7},{7,6},{8,9},{9,8},{10,11... | collective-permute-start | bytes 1572872 | tf_op jit(solution)/shard_map/ppermute | solution.py:37
  245.6 16.6 %collective-permute-start.21 = (bf16[128,2048]{0,1:T(8,128)(2,1)}, bf16[128,2048]{0,1:T(8,128)(2,1)}, u32[]{:S(2)}, u32[]{:S(2)}) collective-permute-start(bf16[128,2048]{0,1:T(8,128)(2,1)} %add_convert_fusion.8), channel_id=1, source_target_pairs={{0,2},{2,0},{1,3},{3,1},{4,6},{6,4},{5,7},{7,5},{8,10},{10,8},{9,1... | collective-permute-start | bytes 1572872 | tf_op jit(solution)/shard_map/ppermute | solution.py:41
  247.2 12.7 %collective-permute-start.23 = (bf16[1,512]{1,0:T(2,128)(2,1)S(1)}, bf16[1,512]{1,0:T(2,128)(2,1)S(1)}, u32[]{:S(2)}, u32[]{:S(2)}) collective-permute-start(bf16[1,512]{1,0:T(2,128)(2,1)S(1)} %get-tuple-element.78), channel_id=1, source_target_pairs={{0,2},{2,0},{1,3},{3,1},{4,6},{6,4},{5,7},{7,5},{8,10},{10,8},{9,1... | collective-permute-start | bytes 3080 | tf_op jit(solution)/shard_map/ppermute | solution.py:41
  247.7 13.6 %collective-permute-start.22 = (bf16[1,512]{1,0:T(2,128)(2,1)S(1)}, bf16[1,512]{1,0:T(2,128)(2,1)S(1)}, u32[]{:S(2)}, u32[]{:S(2)}) collective-permute-start(bf16[1,512]{1,0:T(2,128)(2,1)S(1)} %get-tuple-element.78), channel_id=1, source_target_pairs={{0,1},{1,0},{2,3},{3,2},{4,5},{5,4},{6,7},{7,6},{8,9},{9,8},{10,11... | collective-permute-start | bytes 3080 | tf_op jit(solution)/shard_map/ppermute | solution.py:37
  259.9 2.0 collective-permute-start.24
  266.0 14.4 %collective-permute-start.26 = (bf16[128,2048]{0,1:T(8,128)(2,1)S(1)}, bf16[128,2048]{0,1:T(8,128)(2,1)S(1)}, u32[]{:S(2)}, u32[]{:S(2)}) collective-permute-start(bf16[128,2048]{0,1:T(8,128)(2,1)S(1)} %get-tuple-element.33), channel_id=1, source_target_pairs={{0,2},{2,0},{1,3},{3,1},{4,6},{6,4},{5,7},{7,5},{8,10},{10,8},{9,1... | collective-permute-start | bytes 1572872 | tf_op jit(solution)/shard_map/ppermute | solution.py:41
  267.7 12.8 %collective-permute-start.25 = (bf16[128,2048]{0,1:T(8,128)(2,1)S(1)}, bf16[128,2048]{0,1:T(8,128)(2,1)S(1)}, u32[]{:S(2)}, u32[]{:S(2)}) collective-permute-start(bf16[128,2048]{0,1:T(8,128)(2,1)S(1)} %get-tuple-element.33), channel_id=1, source_target_pairs={{0,1},{1,0},{2,3},{3,2},{4,5},{5,4},{6,7},{7,6},{8,9},{9,8},{10,11... | collective-permute-start | bytes 1572872 | tf_op jit(solution)/shard_map/ppermute | solution.py:37
  315.6 2.0 collective-permute-start.29
  315.8 3.6 collective-permute-start.28
  317.7 14.0 %collective-permute-start.30 = (bf16[512,512]{0,1:T(8,128)(2,1)S(1)}, bf16[512,512]{0,1:T(8,128)(2,1)S(1)}, u32[]{:S(2)}, u32[]{:S(2)}) collective-permute-start(bf16[512,512]{0,1:T(8,128)(2,1)S(1)} %add_convert_fusion.6), channel_id=1, source_target_pairs={{0,2},{2,0},{1,3},{3,1},{4,6},{6,4},{5,7},{7,5},{8,10},{10,8},{9,1... | collective-permute-start | bytes 1572872 | tf_op jit(solution)/shard_map/ppermute | solution.py:41
  333.4 3.6 collective-permute-start.32
  342.2 2.0 collective-permute-start.34
  342.3 3.7 collective-permute-start.33
  344.4 14.0 %collective-permute-start.35 = (bf16[512,512]{1,0:T(8,128)(2,1)S(1)}, bf16[512,512]{1,0:T(8,128)(2,1)S(1)}, u32[]{:S(2)}, u32[]{:S(2)}) collective-permute-start(bf16[512,512]{1,0:T(8,128)(2,1)S(1)} %add_convert_fusion.5), channel_id=1, source_target_pairs={{0,2},{2,0},{1,3},{3,1},{4,6},{6,4},{5,7},{7,5},{8,10},{10,8},{9,1... | collective-permute-start | bytes 1572872 | tf_op jit(solution)/shard_map/ppermute | solution.py:41
  407.2 40.6 %all-to-all-start.3 = ((bf16[8,3,128,256]{2,3,1,0:T(8,128)(2,1)}), bf16[8,3,128,256]{2,3,1,0:T(8,128)(2,1)}, u32[]{:S(2)}, u32[]{:S(2)}) async-start(bf16[8,3,128,256]{2,3,1,0:T(8,128)(2,1)} %copy.187), calls=%async_computation.3 | async-start | bytes 3145728 | tf_op jit(solution)/shard_map/all_to_all | solution.py:180
  411.7 233.1 %all-reduce.3.cloned.1.call-start = ((), (), s32[]{:S(2)}) async-start(), calls=%async_computation.4 | async-start | bytes 6029312 | tf_op jit(solution)/shard_map/psum | solution.py:322
  414.0 3.9 collective-permute-start.54
  419.1 7.9 %collective-permute-start.51 = (f32[512,16]{0,1:T(8,128)}, f32[512,16]{0,1:T(8,128)}, u32[]{:S(2)}, u32[]{:S(2)}) collective-permute-start(f32[512,16]{0,1:T(8,128)} %reduce_sum.168), channel_id=1, source_target_pairs={{0,1},{1,0},{2,3},{3,2},{4,5},{5,4},{6,7},{7,6},{8,9},{9,8},{10,11... | collective-permute-start | bytes 98312 | tf_op jit(solution)/shard_map/ppermute | solution.py:37
  419.1 10.3 %collective-permute-start.49 = (f32[512,16]{0,1:T(8,128)S(1)}, f32[512,16]{0,1:T(8,128)S(1)}, u32[]{:S(2)}, u32[]{:S(2)}) collective-permute-start(f32[512,16]{0,1:T(8,128)S(1)} %reduce_sum.167), channel_id=1, source_target_pairs={{0,1},{1,0},{2,3},{3,2},{4,5},{5,4},{6,7},{7,6},{8,9},{9,8},{10,11... | collective-permute-start | bytes 98312 | tf_op jit(solution)/shard_map/ppermute | solution.py:37
  424.5 5.5 collective-permute-start.47
  427.9 6.1 collective-permute-start.52
  429.5 5.1 collective-permute-start.50
  430.0 12.5 %collective-permute-start.48 = (f32[512,16]{0,1:T(8,128)S(1)}, f32[512,16]{0,1:T(8,128)S(1)}, u32[]{:S(2)}, u32[]{:S(2)}) collective-permute-start(f32[512,16]{0,1:T(8,128)S(1)} %add.424), channel_id=1, source_target_pairs={{0,2},{2,0},{1,3},{3,1},{4,6},{6,4},{5,7},{7,5},{8,10},{10,8},{9,1... | collective-permute-start | bytes 98312 | tf_op jit(solution)/shard_map/ppermute | solution.py:41
  469.9 5.1 collective-permute-start.36
  475.0 3.7 collective-permute-start.37
  477.6 22.5 %collective-permute-start.45 = (f32[512,16]{0,1:T(8,128)}, f32[512,16]{0,1:T(8,128)}, u32[]{:S(2)}, u32[]{:S(2)}) collective-permute-start(f32[512,16]{0,1:T(8,128)} %reduce_sum.165), channel_id=1, source_target_pairs={{0,1},{1,0},{2,3},{3,2},{4,5},{5,4},{6,7},{7,6},{8,9},{9,8},{10,11... | collective-permute-start | bytes 98312 | tf_op jit(solution)/shard_map/ppermute | solution.py:37
  494.2 8.2 %collective-permute-start.43 = (f32[512,16]{0,1:T(8,128)}, f32[512,16]{0,1:T(8,128)}, u32[]{:S(2)}, u32[]{:S(2)}) collective-permute-start(f32[512,16]{0,1:T(8,128)} %reduce_sum.164), channel_id=1, source_target_pairs={{0,1},{1,0},{2,3},{3,2},{4,5},{5,4},{6,7},{7,6},{8,9},{9,8},{10,11... | collective-permute-start | bytes 98312 | tf_op jit(solution)/shard_map/ppermute | solution.py:37
  495.7 7.9 %collective-permute-start.41 = (f32[512,16]{0,1:T(8,128)}, f32[512,16]{0,1:T(8,128)S(1)}, u32[]{:S(2)}, u32[]{:S(2)}) collective-permute-start(f32[512,16]{0,1:T(8,128)} %reduce_sum.163), channel_id=1, source_target_pairs={{0,1},{1,0},{2,3},{3,2},{4,5},{5,4},{6,7},{7,6},{8,9},{9,8},{10,11... | collective-permute-start | bytes 98312 | tf_op jit(solution)/shard_map/ppermute | solution.py:37
  500.8 8.2 %collective-permute-start.46 = (f32[512,16]{0,1:T(8,128)S(1)}, f32[512,16]{0,1:T(8,128)S(1)}, u32[]{:S(2)}, u32[]{:S(2)}) collective-permute-start(f32[512,16]{0,1:T(8,128)S(1)} %add.422), channel_id=1, source_target_pairs={{0,2},{2,0},{1,3},{3,1},{4,6},{6,4},{5,7},{7,5},{8,10},{10,8},{9,1... | collective-permute-start | bytes 98312 | tf_op jit(solution)/shard_map/ppermute | solution.py:41
  503.1 5.9 collective-permute-start.44
  503.6 5.4 collective-permute-start.42
  532.2 5.5 collective-permute-start.38
  534.3 14.1 %collective-permute-start.40 = (bf16[128,2048]{1,0:T(8,128)(2,1)S(1)}, bf16[128,2048]{1,0:T(8,128)(2,1)}, u32[]{:S(2)}, u32[]{:S(2)}) collective-permute-start(bf16[128,2048]{1,0:T(8,128)(2,1)S(1)} %add_convert_fusion.3), channel_id=1, source_target_pairs={{0,2},{2,0},{1,3},{3,1},{4,6},{6,4},{5,7},{7,5},{8,10},{10,8},{9,1... | collective-permute-start | bytes 1572872 | tf_op jit(solution)/shard_map/ppermute | solution.py:41
  (117 other events, 1054.9 us)
Sparse Core Ops, SparseCore 0:
  520.7 124.0 all-reduce.2
where the time goes:
time: 666 us; the launch traced here: 656 us
  waiting for transfers between devices  250 us (38%)
  matrix products  167 us (25%)
  local copies, waits for them, and re-layouts  87.8 us (13%)
  other arithmetic  51.1 us (8%)
  starting transfers between devices  46.8 us (7%)
  blocking collectives  37 us (6%)
  between operations  16.2 us (2%)
    dot_general x56, matrix products, dot(): lax.dot_general(left, right, (dims, ((), ())), preferred_element_type=F32)  145 us
    ppermute x22, waiting for transfers between devices, swap_chip(): return lax.ppermute(values, 'wsh', CHIP_SWAP)  102 us
    psum x1, waiting for transfers between devices, per_device(): model_grads = lax.psum(model_grads, 'ctx')  93.8 us
    all_to_all x1, waiting for transfers between devices, to_heads(): lax.all_to_all(shaped, 'ctx', 0, 0, tiled=True, axis_index_groups=ctx_gro...  34 us
    ppermute x22, starting transfers between devices, swap_chip(): return lax.ppermute(values, 'wsh', CHIP_SWAP)  30 us
    unnamed x222, local copies, waits for them, and re-layouts  22.5 us
    dot_general x6, matrix products, batched(): lax.dot_general(left, right, (((lc,), (rc,)), ((0,), (0,))), preferred_el...  21.8 us
    all_to_all x1, blocking collectives, to_heads(): lax.all_to_all(shaped, 'ctx', 0, 0, tiled=True, axis_index_groups=ctx_gro...  18.6 us
  transfers between devices with their start and end apart: 58, of which 27 were waited for; matrix products, arithmetic and copies ran while one was open for 15% of the time, Pallas kernels for 0%

commit v1 on v0

--- a/solution.py
+++ b/solution.py
@@ -1,3 +1,4 @@
+import functools
 import math
 import jax
 import jax.numpy as jnp
@@ -15,6 +16,14 @@
 BF16 = jnp.bfloat16
 CORE_SWAP = ((0, 1), (1, 0), (2, 3), (3, 2))
 CHIP_SWAP = ((0, 2), (2, 0), (1, 3), (3, 1))
+
+
+def build_types(xx, link_axis):
+    tall = jnp.sum(lax.all_gather(xx, axis_name=link_axis), axis=0)
+    return tall
+
+
+set_tokens = functools.partial(build_types, link_axis="ctx")
 
 
 def dot(left, right, dims):
@@ -319,7 +328,7 @@
     model_grads = jnp.stack(
         grad_a_in + [grad_a_out, grad_a_gate, grad_a_up] + grad_b_in + [grad_b_out, grad_b_down]
     )
-    model_grads = lax.psum(model_grads, "ctx")
+    model_grads = set_tokens(model_grads)
     hidden_grads = lax.psum(hidden_grads, "ctx")
     return (result.astype(BF16)[None], grad_inputs[None], model_grads, hidden_grads)
 

time: 666 us -> 781 us (1.17)
  waiting for transfers between devices: 250 us -> 383 us
  matrix products: 167 us -> 141 us
  other arithmetic: 51.1 us -> 66.2 us
    all_gather x0 -> x1, waiting for transfers between devices: none -> 116 us  [build_types(): tall = jnp.sum(lax.all_gather(xx, axis_name=link_axis), axis=0)]
    all_to_all x1, waiting for transfers between devices: 4.69 us -> 32 us  [to_rows(): lax.all_to_all(shaped.transpose(1, 0, 2, 3), 'ctx', 0, 0, tiled=True, axi...]
    dot_general x56, matrix products: 145 us -> 120 us  [dot(): lax.dot_general(left, right, (dims, ((), ())), preferred_element_type=F32)]
    psum x1, waiting for transfers between devices: 93.8 us -> 84.6 us  [per_device(): hidden_grads = lax.psum(hidden_grads, 'ctx')]
    unnamed x222 -> x211, local copies, waits for them, and re-layouts: 22.5 us -> 20.8 us
  transfers between devices with their start and end apart: 58 -> 59, of which waited for: 27 -> 27; matrix products, arithmetic and copies ran while one was open for 15% -> 14% of each run, Pallas kernels for 0% -> 0%
where the time goes in v1:
time: 781 us; the launch traced here: 770 us
  waiting for transfers between devices  383 us (49%)
  matrix products  141 us (18%)
  local copies, waits for them, and re-layouts  81 us (10%)
  other arithmetic  66.2 us (8%)
  starting transfers between devices  45.8 us (6%)
  blocking collectives  36.8 us (5%)
  between operations  16.2 us (2%)
    dot_general x56, matrix products, dot(): lax.dot_general(left, right, (dims, ((), ())), preferred_element_type=F32)  120 us
    all_gather x1, waiting for transfers between devices, build_types(): tall = jnp.sum(lax.all_gather(xx, axis_name=link_axis), axis=0)  116 us
    ppermute x22, waiting for transfers between devices, swap_chip(): return lax.ppermute(values, 'wsh', CHIP_SWAP)  103 us
    psum x1, waiting for transfers between devices, per_device(): hidden_grads = lax.psum(hidden_grads, 'ctx')  84.6 us
    all_to_all x1, waiting for transfers between devices, to_heads(): lax.all_to_all(shaped, 'ctx', 0, 0, tiled=True, axis_index_groups=ctx_gro...  34 us
    all_to_all x1, waiting for transfers between devices, to_rows(): lax.all_to_all(shaped.transpose(1, 0, 2, 3), 'ctx', 0, 0, tiled=True, axi...  32 us
    ppermute x22, starting transfers between devices, swap_chip(): return lax.ppermute(values, 'wsh', CHIP_SWAP)  29.5 us
    dot_general x6, matrix products, batched(): lax.dot_general(left, right, (((lc,), (rc,)), ((0,), (0,))), preferred_el...  21.8 us
  transfers between devices with their start and end apart: 59, of which 27 were waited for; matrix products, arithmetic and copies ran while one was open for 14% of the time, Pallas kernels for 0%

profile of v1, /device:TPU:0, one launch (start us, length us, event | category | flops | bytes accessed | tf_op | source)
XLA Modules:
  0.0 769.9 jit_solution(15394064448804835944)
XLA Ops:
  7.2 3.0 collective-permute-start.4
  19.7 16.3 %collective-permute-done.7 = bf16[7,64,512]{2,1,0:T(8,128)(2,1)} collective-permute-done((bf16[7,64,512]{2,1,0:T(8,128)(2,1)}, bf16[7,64,512]{2,1,0:T(8,128)(2,1)}, u32[]{:S(2)}, u32[]{:S(2)}) %collective-permute-start.7) | collective-permute-done | bytes 458784 | tf_op jit(solution)/shard_map/ppermute | solution.py:50
  64.4 3.7 maximum_bitcast_fusion
  68.1 3.7 copy.160
  71.8 6.4 all-to-all-start
  81.3 34.0 %all-to-all-done = bf16[8,3,128,256]{3,2,1,0:T(8,128)(2,1)} async-done(((bf16[8,3,128,256]{3,2,1,0:T(8,128)(2,1)}), bf16[8,3,128,256]{3,2,1,0:T(8,128)(2,1)}, u32[]{:S(2)}, u32[]{:S(2)}) %all-to-all-start) | async-done | bytes 1572896 | tf_op jit(solution)/shard_map/all_to_all | solution.py:182
  115.3 2.8 copy.161
  118.1 3.7 reshape.481
  121.8 2.6 copy.162
  124.3 3.0 fusion.18
  130.6 4.8 fusion.75
  138.7 18.4 %all_to_all.20 = bf16[8,1,128,256]{2,3,1,0:T(8,128)(2,1)} all-to-all(bf16[8,1,128,256]{2,3,1,0:T(8,128)(2,1)S(1)} %copy.165), channel_id=1, replica_groups={{0,4,8,12,16,20,24,28},{1,5,9,13,17,21,25,29},{2,6,10,14,18,22,26,30},{..., dimensions={0} | all-to-all | bytes 1048576 | tf_op jit(solution)/shard_map/all_to_all | solution.py:189
  164.1 11.1 %collective-permute-done.12 = bf16[512,512]{0,1:T(8,128)(2,1)S(1)} collective-permute-done((bf16[512,512]{0,1:T(8,128)(2,1)S(1)}, bf16[512,512]{0,1:T(8,128)(2,1)S(1)}, u32[]{:S(2)}, u32[]{:S(2)}) %collective-permute-start.12) | collective-permute-done | bytes 524320 | tf_op jit(solution)/shard_map/ppermute | solution.py:50
  178.6 2.9 multiply_reduce_fusion.5
  189.0 11.3 %collective-permute-done.17 = bf16[512,512]{0,1:T(8,128)(2,1)S(1)} collective-permute-done((bf16[512,512]{0,1:T(8,128)(2,1)S(1)}, bf16[512,512]{0,1:T(8,128)(2,1)S(1)}, u32[]{:S(2)}, u32[]{:S(2)}) %collective-permute-start.17) | collective-permute-done | bytes 524320 | tf_op jit(solution)/shard_map/ppermute | solution.py:50
  205.6 11.6 %multiply_add_fusion.1 = f32[512,2048]{0,1:T(8,128)} fusion(f32[512,2048]{0,1:T(8,128)S(1)} %fusion.137, bf16[512,2048]{0,1:T(8,128)(2,1)S(1)} %constant_dynamic-update-slice_fusion.4, bf16[3,2048,2048]{2,1,0:T(8,128)(2,1)} %param.13), kind=kOutput, calls=%fused_computation.37 | convolution fusion | flops 4297064448 | bytes 18874368 | tf_op jit(solution)/shard_map/dot_general | solution.py:30
  217.1 13.1 %multiply_convert_fusion.3 = (bf16[512,2048]{0,1:T(8,128)(2,1)S(1)}, f32[512,2048]{0,1:T(8,128)}) fusion(f32[512,2048]{0,1:T(8,128)} %multiply_add_fusion.1, f32[512,2048]{0,1:T(8,128)S(1)} %fusion.134, bf16[512,2048]{0,1:T(8,128)(2,1)S(1)} %constant_dynamic-update-slice_fusion.4, bf16[3,2048,2048]{2,1,0:T(8,128)(2,1)} %param.13), kind=kOutput, calls=%fused_computation.33 | convolution fusion | flops 4303355904 | bytes 25165824 | tf_op jit(solution)/shard_map/dot_general | solution.py:30
  230.7 7.2 fusion.2
  247.1 10.0 %collective-permute-done.23 = bf16[1,512]{1,0:T(2,128)(2,1)S(1)} collective-permute-done((bf16[1,512]{1,0:T(2,128)(2,1)S(1)}, bf16[1,512]{1,0:T(2,128)(2,1)S(1)}, u32[]{:S(2)}, u32[]{:S(2)}) %collective-permute-start.23) | collective-permute-done | bytes 1056 | tf_op jit(solution)/shard_map/ppermute | solution.py:50
  265.4 12.5 %collective-permute-done.26 = bf16[128,2048]{0,1:T(8,128)(2,1)S(1)} collective-permute-done((bf16[128,2048]{0,1:T(8,128)(2,1)S(1)}, bf16[128,2048]{0,1:T(8,128)(2,1)S(1)}, u32[]{:S(2)}, u32[]{:S(2)}) %collective-permute-start.26) | collective-permute-done | bytes 524320 | tf_op jit(solution)/shard_map/ppermute | solution.py:50
  281.3 9.9 %multiply_convert_fusion.1 = (bf16[512,2048]{0,1:T(8,128)(2,1)S(1)}, bf16[512,2048]{0,1:T(8,128)(2,1)S(1)}) fusion(f32[512,2048]{0,1:T(8,128)} %multiply_add_fusion.1, f32[512,2048]{0,1:T(8,128)} %get-tuple-element.94, f32[512,2048]{0,1:T(8,128)S(1)} %fusion.130, bf16[512,2048]{0,1:T(8,128)(2,1)S(1)} %constant_dynamic-update-slice_fusion, ...), kind=kOutput, calls=%fused_computation.30 | convolution fusion | flops 4309647360 | bytes 27262976 | tf_op jit(solution)/shard_map/dot_general | solution.py:30
  291.7 7.9 %fusion.8 = f32[512,2048]{0,1:T(8,128)S(1)} fusion(bf16[512,2048]{0,1:T(8,128)(2,1)S(1)} %get-tuple-element.37, bf16[3,2048,2048]{2,1,0:T(8,128)(2,1)} %param.13), kind=kOutput, calls=%fused_computation.8 | convolution fusion | flops 4294967296 | bytes 14680064 | tf_op jit(solution)/shard_map/dot_general | solution.py:30
  300.1 6.9 fusion.4
  313.9 12.4 %collective-permute-done.30 = bf16[512,512]{0,1:T(8,128)(2,1)S(1)} collective-permute-done((bf16[512,512]{0,1:T(8,128)(2,1)S(1)}, bf16[512,512]{0,1:T(8,128)(2,1)S(1)}, u32[]{:S(2)}, u32[]{:S(2)}) %collective-permute-start.30) | collective-permute-done | bytes 524320 | tf_op jit(solution)/shard_map/ppermute | solution.py:50
  332.0 3.0 fusion.32
  339.6 12.4 %collective-permute-done.35 = bf16[512,512]{1,0:T(8,128)(2,1)S(1)} collective-permute-done((bf16[512,512]{1,0:T(8,128)(2,1)S(1)}, bf16[512,512]{1,0:T(8,128)(2,1)S(1)}, u32[]{:S(2)}, u32[]{:S(2)}) %collective-permute-start.35) | collective-permute-done | bytes 524320 | tf_op jit(solution)/shard_map/ppermute | solution.py:50
  356.2 18.4 %all_to_all.21 = bf16[8,1,128,256]{3,2,1,0:T(8,128)(2,1)} all-to-all(bf16[8,1,128,256]{3,2,1,0:T(8,128)(2,1)S(1)} %bitcast.548), channel_id=1, replica_groups={{0,4,8,12,16,20,24,28},{1,5,9,13,17,21,25,29},{2,6,10,14,18,22,26,30},{..., dimensions={0} | all-to-all | bytes 1048576 | tf_op jit(solution)/shard_map/all_to_all | solution.py:182
  376.5 5.5 fusion.76
  382.1 5.5 multiply_reduce_fusion
  387.6 2.7 multiply_convert_fusion
  394.7 2.6 copy.186
  400.6 4.4 all-to-all-start.3
  409.2 32.0 %all-to-all-done.3 = bf16[8,3,128,256]{2,3,1,0:T(8,128)(2,1)} async-done(((bf16[8,3,128,256]{2,3,1,0:T(8,128)(2,1)}), bf16[8,3,128,256]{2,3,1,0:T(8,128)(2,1)}, u32[]{:S(2)}, u32[]{:S(2)}) %all-to-all-start.3) | async-done | bytes 1572896 | tf_op jit(solution)/shard_map/all_to_all | solution.py:189
  441.2 3.0 copy.188
  444.1 2.7 fusion.192
  449.8 2.6 copy.189
  452.4 2.6 reshape.498
  506.5 3.2 convolution_bitcast_fusion
  509.7 3.1 fusion.31
  515.9 3.0 fusion.36
  520.8 3.6 fusion.140
  527.1 4.3 add_convert_fusion
  540.1 9.8 %collective-permute-done.40 = bf16[128,2048]{1,0:T(8,128)(2,1)} collective-permute-done((bf16[128,2048]{1,0:T(8,128)(2,1)S(1)}, bf16[128,2048]{1,0:T(8,128)(2,1)}, u32[]{:S(2)}, u32[]{:S(2)}) %collective-permute-start.40) | collective-permute-done | bytes 524320 | tf_op jit(solution)/shard_map/ppermute | solution.py:50
  550.0 2.4 add_bitcast_fusion
  552.4 116.2 %all-gather.3.cloned.1.call-done = f32[88,64,512]{2,1,0:T(8,128)} async-done(((f32[11,64,512]{2,1,0:T(8,128)}), f32[88,64,512]{2,1,0:T(8,128)}) %all-gather.3.cloned.1.call-update) | async-done | bytes 11534352 | tf_op jit(solution)/shard_map/all_gather | solution.py:22
  668.6 6.9 reduce_sum.179
  675.5 84.6 %all-reduce.2.cloned.1.call-done = f32[3,64,2048]{2,1,0:T(8,128)} async-done(((f32[3,64,2048]{2,1,0:T(8,128)}), f32[3,64,2048]{2,1,0:T(8,128)}) %all-reduce.2.cloned.1.call-update) | async-done | bytes 1572880 | tf_op jit(solution)/shard_map/psum | solution.py:332
  760.1 2.7 copy.295
  (513 shorter events, 197.3 us)
Async XLA Ops:
  7.2 9.8 %collective-permute-start.4 = (s32[1,16]{1,0:T(1,128)}, s32[1,16]{1,0:T(1,128)S(1)}, u32[]{:S(2)}, u32[]{:S(2)}) collective-permute-start(s32[1,16]{1,0:T(1,128)} %param.19), channel_id=1, source_target_pairs={{0,2},{2,0},{1,3},{3,1},{4,6},{6,4},{5,7},{7,5},{8,10},{10,8},{9,1... | collective-permute-start | bytes 200 | tf_op jit(solution)/shard_map/ppermute | solution.py:50
  10.2 4.7 collective-permute-start.3
  11.5 27.8 %collective-permute-start = (bf16[128,2048]{0,1:T(8,128)(2,1)S(1)}, bf16[128,2048]{0,1:T(8,128)(2,1)}, u32[]{:S(2)}, u32[]{:S(2)}) collective-permute-start(bf16[128,2048]{0,1:T(8,128)(2,1)S(1)} %bitcast.543), channel_id=1, source_target_pairs={{0,1},{1,0},{2,3},{3,2},{4,5},{5,4},{6,7},{7,6},{8,9},{9,8},{10,11... | collective-permute-start | bytes 1572872 | tf_op jit(solution)/shard_map/ppermute | solution.py:46
  12.1 26.7 %collective-permute-start.1 = (bf16[128,2048]{0,1:T(8,128)(2,1)S(1)}, bf16[128,2048]{0,1:T(8,128)(2,1)}, u32[]{:S(2)}, u32[]{:S(2)}) collective-permute-start(bf16[128,2048]{0,1:T(8,128)(2,1)S(1)} %bitcast.544), channel_id=1, source_target_pairs={{0,2},{2,0},{1,3},{3,1},{4,6},{6,4},{5,7},{7,5},{8,10},{10,8},{9,1... | collective-permute-start | bytes 1572872 | tf_op jit(solution)/shard_map/ppermute | solution.py:50
  13.3 22.6 %collective-permute-start.6 = (bf16[7,64,512]{2,1,0:T(8,128)(2,1)}, bf16[7,64,512]{2,1,0:T(8,128)(2,1)S(1)}, u32[]{:S(2)}, u32[]{:S(2)}) collective-permute-start(bf16[7,64,512]{2,1,0:T(8,128)(2,1)} %get-tuple-element.57), channel_id=1, source_target_pairs={{0,1},{1,0},{2,3},{3,2},{4,5},{5,4},{6,7},{7,6},{8,9},{9,8},{10,11... | collective-permute-start | bytes 1376264 | tf_op jit(solution)/shard_map/ppermute | solution.py:46
  14.9 21.0 %collective-permute-start.7 = (bf16[7,64,512]{2,1,0:T(8,128)(2,1)}, bf16[7,64,512]{2,1,0:T(8,128)(2,1)}, u32[]{:S(2)}, u32[]{:S(2)}) collective-permute-start(bf16[7,64,512]{2,1,0:T(8,128)(2,1)} %get-tuple-element.57), channel_id=1, source_target_pairs={{0,2},{2,0},{1,3},{3,1},{4,6},{6,4},{5,7},{7,5},{8,10},{10,8},{9,1... | collective-permute-start | bytes 1376264 | tf_op jit(solution)/shard_map/ppermute | solution.py:50
  36.0 5.7 collective-permute-start.8
  38.8 3.7 collective-permute-start.2
  53.6 4.3 collective-permute-start.10
  71.8 43.5 %all-to-all-start = ((bf16[8,3,128,256]{3,2,1,0:T(8,128)(2,1)}), bf16[8,3,128,256]{3,2,1,0:T(8,128)(2,1)}, u32[]{:S(2)}, u32[]{:S(2)}) async-start(bf16[8,3,128,256]{3,2,1,0:T(8,128)(2,1)} %bitcast.532), calls=%async_computation | async-start | bytes 3145728 | tf_op jit(solution)/shard_map/all_to_all | solution.py:182
  162.5 12.7 %collective-permute-start.12 = (bf16[512,512]{0,1:T(8,128)(2,1)S(1)}, bf16[512,512]{0,1:T(8,128)(2,1)S(1)}, u32[]{:S(2)}, u32[]{:S(2)}) collective-permute-start(bf16[512,512]{0,1:T(8,128)(2,1)S(1)} %bitcast.557), channel_id=1, source_target_pairs={{0,2},{2,0},{1,3},{3,1},{4,6},{6,4},{5,7},{7,5},{8,10},{10,8},{9,1... | collective-permute-start | bytes 1572872 | tf_op jit(solution)/shard_map/ppermute | solution.py:50
  164.1 11.3 %collective-permute-start.11 = (bf16[512,512]{0,1:T(8,128)(2,1)S(1)}, bf16[512,512]{0,1:T(8,128)(2,1)S(1)}, u32[]{:S(2)}, u32[]{:S(2)}) collective-permute-start(bf16[512,512]{0,1:T(8,128)(2,1)S(1)} %bitcast.558), channel_id=1, source_target_pairs={{0,1},{1,0},{2,3},{3,2},{4,5},{5,4},{6,7},{7,6},{8,9},{9,8},{10,11... | collective-permute-start | bytes 1572872 | tf_op jit(solution)/shard_map/ppermute | solution.py:46
  182.8 3.6 collective-permute-start.15
  187.5 12.9 %collective-permute-start.17 = (bf16[512,512]{0,1:T(8,128)(2,1)S(1)}, bf16[512,512]{0,1:T(8,128)(2,1)S(1)}, u32[]{:S(2)}, u32[]{:S(2)}) collective-permute-start(bf16[512,512]{0,1:T(8,128)(2,1)S(1)} %get-tuple-element.33), channel_id=1, source_target_pairs={{0,2},{2,0},{1,3},{3,1},{4,6},{6,4},{5,7},{7,5},{8,10},{10,8},{9,1... | collective-permute-start | bytes 1572872 | tf_op jit(solution)/shard_map/ppermute | solution.py:50
  189.0 11.3 %collective-permute-start.16 = (bf16[512,512]{0,1:T(8,128)(2,1)S(1)}, bf16[512,512]{0,1:T(8,128)(2,1)S(1)}, u32[]{:S(2)}, u32[]{:S(2)}) collective-permute-start(bf16[512,512]{0,1:T(8,128)(2,1)S(1)} %get-tuple-element.33), channel_id=1, source_target_pairs={{0,1},{1,0},{2,3},{3,2},{4,5},{5,4},{6,7},{7,6},{8,9},{9,8},{10,11... | collective-permute-start | bytes 1572872 | tf_op jit(solution)/shard_map/ppermute | solution.py:46
  240.0 19.4 %collective-permute-start.19 = (bf16[128,2048]{0,1:T(8,128)(2,1)}, bf16[128,2048]{0,1:T(8,128)(2,1)}, u32[]{:S(2)}, u32[]{:S(2)}) collective-permute-start(bf16[128,2048]{0,1:T(8,128)(2,1)} %get-tuple-element.44), channel_id=1, source_target_pairs={{0,1},{1,0},{2,3},{3,2},{4,5},{5,4},{6,7},{7,6},{8,9},{9,8},{10,11... | collective-permute-start | bytes 1572872 | tf_op jit(solution)/shard_map/ppermute | solution.py:46
  242.8 16.6 %collective-permute-start.21 = (bf16[128,2048]{0,1:T(8,128)(2,1)}, bf16[128,2048]{0,1:T(8,128)(2,1)}, u32[]{:S(2)}, u32[]{:S(2)}) collective-permute-start(bf16[128,2048]{0,1:T(8,128)(2,1)} %add_convert_fusion.8), channel_id=1, source_target_pairs={{0,2},{2,0},{1,3},{3,1},{4,6},{6,4},{5,7},{7,5},{8,10},{10,8},{9,1... | collective-permute-start | bytes 1572872 | tf_op jit(solution)/shard_map/ppermute | solution.py:50
  244.3 12.8 %collective-permute-start.23 = (bf16[1,512]{1,0:T(2,128)(2,1)S(1)}, bf16[1,512]{1,0:T(2,128)(2,1)S(1)}, u32[]{:S(2)}, u32[]{:S(2)}) collective-permute-start(bf16[1,512]{1,0:T(2,128)(2,1)S(1)} %get-tuple-element.76), channel_id=1, source_target_pairs={{0,2},{2,0},{1,3},{3,1},{4,6},{6,4},{5,7},{7,5},{8,10},{10,8},{9,1... | collective-permute-start | bytes 3080 | tf_op jit(solution)/shard_map/ppermute | solution.py:50
  244.9 13.6 %collective-permute-start.22 = (bf16[1,512]{1,0:T(2,128)(2,1)S(1)}, bf16[1,512]{1,0:T(2,128)(2,1)S(1)}, u32[]{:S(2)}, u32[]{:S(2)}) collective-permute-start(bf16[1,512]{1,0:T(2,128)(2,1)S(1)} %get-tuple-element.76), channel_id=1, source_target_pairs={{0,1},{1,0},{2,3},{3,2},{4,5},{5,4},{6,7},{7,6},{8,9},{9,8},{10,11... | collective-permute-start | bytes 3080 | tf_op jit(solution)/shard_map/ppermute | solution.py:46
  263.5 14.4 %collective-permute-start.26 = (bf16[128,2048]{0,1:T(8,128)(2,1)S(1)}, bf16[128,2048]{0,1:T(8,128)(2,1)S(1)}, u32[]{:S(2)}, u32[]{:S(2)}) collective-permute-start(bf16[128,2048]{0,1:T(8,128)(2,1)S(1)} %get-tuple-element.31), channel_id=1, source_target_pairs={{0,2},{2,0},{1,3},{3,1},{4,6},{6,4},{5,7},{7,5},{8,10},{10,8},{9,1... | collective-permute-start | bytes 1572872 | tf_op jit(solution)/shard_map/ppermute | solution.py:50
  265.1 12.9 %collective-permute-start.25 = (bf16[128,2048]{0,1:T(8,128)(2,1)S(1)}, bf16[128,2048]{0,1:T(8,128)(2,1)S(1)}, u32[]{:S(2)}, u32[]{:S(2)}) collective-permute-start(bf16[128,2048]{0,1:T(8,128)(2,1)S(1)} %get-tuple-element.31), channel_id=1, source_target_pairs={{0,1},{1,0},{2,3},{3,2},{4,5},{5,4},{6,7},{7,6},{8,9},{9,8},{10,11... | collective-permute-start | bytes 1572872 | tf_op jit(solution)/shard_map/ppermute | solution.py:46
  310.4 3.6 collective-permute-start.28
  312.3 14.0 %collective-permute-start.30 = (bf16[512,512]{0,1:T(8,128)(2,1)S(1)}, bf16[512,512]{0,1:T(8,128)(2,1)S(1)}, u32[]{:S(2)}, u32[]{:S(2)}) collective-permute-start(bf16[512,512]{0,1:T(8,128)(2,1)S(1)} %add_convert_fusion.6), channel_id=1, source_target_pairs={{0,2},{2,0},{1,3},{3,1},{4,6},{6,4},{5,7},{7,5},{8,10},{10,8},{9,1... | collective-permute-start | bytes 1572872 | tf_op jit(solution)/shard_map/ppermute | solution.py:50
  327.9 3.6 collective-permute-start.32
  335.9 3.7 collective-permute-start.33
  338.0 14.0 %collective-permute-start.35 = (bf16[512,512]{1,0:T(8,128)(2,1)S(1)}, bf16[512,512]{1,0:T(8,128)(2,1)S(1)}, u32[]{:S(2)}, u32[]{:S(2)}) collective-permute-start(bf16[512,512]{1,0:T(8,128)(2,1)S(1)} %add_convert_fusion.5), channel_id=1, source_target_pairs={{0,2},{2,0},{1,3},{3,1},{4,6},{6,4},{5,7},{7,5},{8,10},{10,8},{9,1... | collective-permute-start | bytes 1572872 | tf_op jit(solution)/shard_map/ppermute | solution.py:50
  400.6 40.6 %all-to-all-start.3 = ((bf16[8,3,128,256]{2,3,1,0:T(8,128)(2,1)}), bf16[8,3,128,256]{2,3,1,0:T(8,128)(2,1)}, u32[]{:S(2)}, u32[]{:S(2)}) async-start(bf16[8,3,128,256]{2,3,1,0:T(8,128)(2,1)} %copy.187), calls=%async_computation.3 | async-start | bytes 3145728 | tf_op jit(solution)/shard_map/all_to_all | solution.py:189
  405.0 263.5 %all-gather.3.cloned.1.call-start = ((), (), s32[]{:S(2)}) async-start(), calls=%async_computation.5 | async-start | bytes 12976128 | tf_op jit(solution)/shard_map/all_gather | solution.py:22
  406.3 53.9 %collective-permute-start.53 = (f32[512,16]{0,1:T(8,128)}, f32[512,16]{0,1:T(8,128)}, u32[]{:S(2)}, u32[]{:S(2)}) collective-permute-start(f32[512,16]{0,1:T(8,128)} %reduce_sum.178), channel_id=1, source_target_pairs={{0,1},{1,0},{2,3},{3,2},{4,5},{5,4},{6,7},{7,6},{8,9},{9,8},{10,11... | collective-permute-start | bytes 98312 | tf_op jit(solution)/shard_map/ppermute | solution.py:46
  406.9 56.3 %collective-permute-start.51 = (f32[512,16]{0,1:T(8,128)}, f32[512,16]{0,1:T(8,128)}, u32[]{:S(2)}, u32[]{:S(2)}) collective-permute-start(f32[512,16]{0,1:T(8,128)} %reduce_sum.177), channel_id=1, source_target_pairs={{0,1},{1,0},{2,3},{3,2},{4,5},{5,4},{6,7},{7,6},{8,9},{9,8},{10,11... | collective-permute-start | bytes 98312 | tf_op jit(solution)/shard_map/ppermute | solution.py:46
  408.0 57.0 %collective-permute-start.49 = (f32[512,16]{0,1:T(8,128)}, f32[512,16]{0,1:T(8,128)}, u32[]{:S(2)}, u32[]{:S(2)}) collective-permute-start(f32[512,16]{0,1:T(8,128)} %reduce_sum.176), channel_id=1, source_target_pairs={{0,1},{1,0},{2,3},{3,2},{4,5},{5,4},{6,7},{7,6},{8,9},{9,8},{10,11... | collective-permute-start | bytes 98312 | tf_op jit(solution)/shard_map/ppermute | solution.py:46
  408.7 59.3 %collective-permute-start.47 = (f32[512,16]{0,1:T(8,128)}, f32[512,16]{0,1:T(8,128)}, u32[]{:S(2)}, u32[]{:S(2)}) collective-permute-start(f32[512,16]{0,1:T(8,128)} %reduce_sum.175), channel_id=1, source_target_pairs={{0,1},{1,0},{2,3},{3,2},{4,5},{5,4},{6,7},{7,6},{8,9},{9,8},{10,11... | collective-permute-start | bytes 98312 | tf_op jit(solution)/shard_map/ppermute | solution.py:46
  459.6 10.9 %collective-permute-start.36 = (f32[2,512]{1,0:T(2,128)S(1)}, f32[2,512]{1,0:T(2,128)S(1)}, u32[]{:S(2)}, u32[]{:S(2)}) collective-permute-start(f32[2,512]{1,0:T(2,128)S(1)} %pad_maximum_fusion.7), channel_id=1, source_target_pairs={{0,1},{1,0},{2,3},{3,2},{4,5},{5,4},{6,7},{7,6},{8,9},{9,8},{10,11... | collective-permute-start | bytes 12296 | tf_op jit(solution)/shard_map/ppermute | solution.py:46
  461.6 18.8 %collective-permute-start.54 = (f32[512,16]{0,1:T(8,128)}, f32[512,16]{0,1:T(8,128)}, u32[]{:S(2)}, u32[]{:S(2)}) collective-permute-start(f32[512,16]{0,1:T(8,128)} %add.428), channel_id=1, source_target_pairs={{0,2},{2,0},{1,3},{3,1},{4,6},{6,4},{5,7},{7,5},{8,10},{10,8},{9,1... | collective-permute-start | bytes 98312 | tf_op jit(solution)/shard_map/ppermute | solution.py:50
  464.6 17.9 %collective-permute-start.52 = (f32[512,16]{0,1:T(8,128)}, f32[512,16]{0,1:T(8,128)}, u32[]{:S(2)}, u32[]{:S(2)}) collective-permute-start(f32[512,16]{0,1:T(8,128)} %add.426), channel_id=1, source_target_pairs={{0,2},{2,0},{1,3},{3,1},{4,6},{6,4},{5,7},{7,5},{8,10},{10,8},{9,1... | collective-permute-start | bytes 98312 | tf_op jit(solution)/shard_map/ppermute | solution.py:50
  466.4 18.3 %collective-permute-start.50 = (f32[512,16]{0,1:T(8,128)}, f32[512,16]{0,1:T(8,128)}, u32[]{:S(2)}, u32[]{:S(2)}) collective-permute-start(f32[512,16]{0,1:T(8,128)} %add.424), channel_id=1, source_target_pairs={{0,2},{2,0},{1,3},{3,1},{4,6},{6,4},{5,7},{7,5},{8,10},{10,8},{9,1... | collective-permute-start | bytes 98312 | tf_op jit(solution)/shard_map/ppermute | solution.py:50
  469.4 16.2 %collective-permute-start.48 = (f32[512,16]{0,1:T(8,128)}, f32[512,16]{0,1:T(8,128)}, u32[]{:S(2)}, u32[]{:S(2)}) collective-permute-start(f32[512,16]{0,1:T(8,128)} %add.422), channel_id=1, source_target_pairs={{0,2},{2,0},{1,3},{3,1},{4,6},{6,4},{5,7},{7,5},{8,10},{10,8},{9,1... | collective-permute-start | bytes 98312 | tf_op jit(solution)/shard_map/ppermute | solution.py:50
  470.5 3.7 collective-permute-start.37
  474.2 12.1 %collective-permute-start.45 = (f32[512,16]{0,1:T(8,128)}, f32[512,16]{0,1:T(8,128)}, u32[]{:S(2)}, u32[]{:S(2)}) collective-permute-start(f32[512,16]{0,1:T(8,128)} %reduce_sum.174), channel_id=1, source_target_pairs={{0,1},{1,0},{2,3},{3,2},{4,5},{5,4},{6,7},{7,6},{8,9},{9,8},{10,11... | collective-permute-start | bytes 98312 | tf_op jit(solution)/shard_map/ppermute | solution.py:46
  480.4 8.3 %collective-permute-start.43 = (f32[512,16]{0,1:T(8,128)}, f32[512,16]{0,1:T(8,128)}, u32[]{:S(2)}, u32[]{:S(2)}) collective-permute-start(f32[512,16]{0,1:T(8,128)} %reduce_sum.173), channel_id=1, source_target_pairs={{0,1},{1,0},{2,3},{3,2},{4,5},{5,4},{6,7},{7,6},{8,9},{9,8},{10,11... | collective-permute-start | bytes 98312 | tf_op jit(solution)/shard_map/ppermute | solution.py:46
  482.4 7.6 collective-permute-start.41
  487.1 6.1 collective-permute-start.46
  489.5 4.1 collective-permute-start.44
  490.8 3.9 collective-permute-start.42
  506.2 254.0 %all-reduce.2.cloned.1.call-start = ((), (), s32[]{:S(2)}) async-start(), calls=%async_computation.4 | async-start | bytes 3145728 | tf_op jit(solution)/shard_map/psum | solution.py:332
  532.3 3.1 collective-permute-start.39
  535.3 4.9 collective-permute-start.38
  535.5 14.5 %collective-permute-start.40 = (bf16[128,2048]{1,0:T(8,128)(2,1)S(1)}, bf16[128,2048]{1,0:T(8,128)(2,1)}, u32[]{:S(2)}, u32[]{:S(2)}) collective-permute-start(bf16[128,2048]{1,0:T(8,128)(2,1)S(1)} %add_convert_fusion.3), channel_id=1, source_target_pairs={{0,2},{2,0},{1,3},{3,1},{4,6},{6,4},{5,7},{7,5},{8,10},{10,8},{9,1... | collective-permute-start | bytes 1572872 | tf_op jit(solution)/shard_map/ppermute | solution.py:50
  (113 other events, 887.5 us)
Sparse Core Ops, SparseCore 0:
  506.3 162.2 all-gather.2
  672.7 87.4 all-reduce.1
